TPU v7x, 256 devices: a whole 4x4x8 slice. The times are simulated.
256 devices in a mesh: freq: 4 (over y_hi, core), sub: 64 (over x, z, y_lo).
Axes of the slice: x: 4, y: 4 (y_hi: 2, y_lo: 2; y = y_hi * 2 + y_lo), z: 8, core: 2. Of those that a mesh axis runs over, the one named last changes fastest.
Arguments:
- impedance: float32 [4, 64, 1280, 1280], P('freq', 'sub'), may hold values from -0.125 to 0.125
- interior_map: bfloat16 [4, 64, 2048, 1280], P('freq', 'sub'), may hold values from -6 to 6
- source_cells: int32 [128], replicated, may hold values from 0 to 65535
- receiver_cells: int32 [128], replicated, may hold values from 0 to 65535
Outputs:
- hessian: float32 [64, 1024, 1024], P('sub', 'freq')
All inputs are finite; a program needn't handle non-finite values.
Results may differ from a plain program's by a relative error of at most 0.0059.
Values may be sent and summed in bfloat16 or wider, within the bound.
A program may use at most 64 MiB of HBM per device.

v0:
```python
import jax
import jax.numpy as jnp
from jax import lax
from jax.sharding import PartitionSpec as P

CX = 8
CY = 8
CZ = 16
NSRC = 128
NRCV = 128
SWEEPS = 3
CELLS = 1024
FACES = 640
TRACE = 1280
RHS = 256


def shifted(value, axis, by):
    size = lax.axis_size(axis)
    pairs = [(i, i + by) for i in range(size) if 0 <= i + by < size]
    return lax.ppermute(value, axis, pairs)


def face_spans(cells_x, cells_y, cells_z):
    counts = [
        cells_y * cells_z,
        cells_y * cells_z,
        cells_x * cells_z,
        cells_x * cells_z,
        cells_x * cells_y,
        cells_x * cells_y,
    ]
    spans = []
    begin = 0
    for count in counts:
        spans.append((begin, count))
        begin = begin + count
    return spans


def gram_rows(fields, first, count):
    cells = fields.shape[0] // 2
    real_part = fields[:cells, first : first + count]
    imag_part = fields[cells:, first : first + count]
    left = jnp.concatenate([real_part, imag_part], axis=1)
    rotated_block = jnp.concatenate([imag_part, -real_part], axis=1)
    dims = (((1,), (1,)), ((), ()))
    real_gram = lax.dot_general(left, left, dims, preferred_element_type=jnp.float32)
    imaginary_gram_matrix = lax.dot_general(
        rotated_block, left, dims, preferred_element_type=jnp.float32
    )
    return (real_gram, imaginary_gram_matrix)


def hessian_terms(fields):
    real_u, imag_u = gram_rows(fields, 0, NSRC)
    real_v, imag_v = gram_rows(fields, NSRC, NRCV)
    return (real_u * real_v - imag_u * imag_v) / (NSRC * NRCV)


def swap_faces(outgoing_trace_values, coords, grid_sizes, strides):
    stacked = outgoing_trace_values.reshape(2, FACES, RHS)
    spans = face_spans(CX, CY, CZ)
    pieces = []
    for face_index in range(6):
        axis_number = face_index // 2
        partner = face_index + 1 if face_index % 2 == 0 else face_index - 1
        begin, count = spans[partner]
        piece = stacked[:, begin : begin + count, :]
        if face_index % 2 == 0:
            offset = strides[axis_number]
            valid = coords[axis_number] > 0
        else:
            offset = -strides[axis_number]
            valid = coords[axis_number] < grid_sizes[axis_number] - 1
        arrived = shifted(piece, "sub", offset)
        pieces.append(jnp.where(valid, arrived, jnp.float32(0.0)))
    return jnp.concatenate(pieces, axis=1).reshape(TRACE, RHS)


def local(impedance, interior_map, source_cells, receiver_cells):
    operator = impedance[0, 0]
    interior = interior_map[0, 0]
    nsub = lax.axis_size("sub")
    grid_x = min(4, nsub)
    grid_y = min(4, nsub // grid_x)
    grid_z = nsub // (grid_x * grid_y)
    cell_position = lax.axis_index("sub")
    coords = (
        cell_position % grid_x,
        cell_position // grid_x % grid_y,
        cell_position // (grid_x * grid_y),
    )
    grid_sizes = (grid_x, grid_y, grid_z)
    strides = (1, grid_x, grid_x * grid_y)
    all_cells = jnp.concatenate([source_cells, receiver_cells])
    inside = all_cells // CELLS == cell_position
    local_cell = all_cells % CELLS
    picked = jnp.take(interior, local_cell, axis=0).astype(jnp.float32)
    source_loading = jnp.where(inside[:, None], picked, jnp.float32(0.0)).T
    incoming_trace_values = jnp.zeros((TRACE, RHS), jnp.float32)
    for sweep_index in range(SWEEPS):
        outgoing_trace_values = (
            jnp.dot(operator, incoming_trace_values, precision=lax.Precision.HIGHEST)
            + source_loading
        )
        incoming_trace_values = swap_faces(outgoing_trace_values, coords, grid_sizes, strides)
    product = jnp.dot(
        interior, incoming_trace_values.astype(jnp.bfloat16), preferred_element_type=jnp.float32
    )
    row_ids = jnp.arange(2 * CELLS, dtype=jnp.int32)
    point = (row_ids[:, None] == local_cell[None, :]) & inside[None, :]
    field_scale = jnp.float32(TRACE ** (-0.5))
    fields = (product * field_scale + point.astype(jnp.float32)).astype(jnp.bfloat16)
    owned = lax.psum_scatter(hessian_terms(fields), "freq", scatter_dimension=0, tiled=True)
    return owned[None]


def solution(mesh):
    in_specs = (P("freq", "sub", None, None), P("freq", "sub", None, None), P(), P())
    out_specs = P("sub", "freq", None)
    return jax.shard_map(local, mesh=mesh, in_specs=in_specs, out_specs=out_specs, check_vma=False)
```

profile of v0, /device:TPU:35, one launch (start us, length us, event | category | flops | bytes accessed | tf_op | source)
XLA Modules:
  0.0 222.5 jit_solution(9321894066827788506)
XLA Ops:
  8.6 4.9 %gather_fusion = bf16[256,1280]{1,0:T(8,128)(2,1)S(1)} fusion(bf16[2048,1280]{1,0:T(8,128)(2,1)} %bitcast.61, s32[1024]{0:T(1024)S(1)} %pad_clamp_fusion), kind=kCustom, calls=%fused_computation | custom fusion | bytes 1311744 | tf_op jit(solution)/shard_map/jit(_take)/gather | solution.py:99
  13.5 8.3 %fusion.22 = f32[1280,256]{0,1:T(8,128)S(1)} fusion(f32[1,1,1280,1280]{3,2,1,0:T(8,128)} %param.4, pred[256]{0:T(512)(128)(4,1)S(1)} %get-tuple-element.31, bf16[256,1280]{1,0:T(8,128)(2,1)S(1)} %gather_fusion, pred[256]{0:T(512)(128)(4,1)S(1)} %get-tuple-element.5), kind=kOutput, calls=%fused_computation.15 | convolution fusion | flops 5034475520 | bytes 8520192 | tf_op jit(solution)/shard_map/dot_general | solution.py:104
  25.0 3.1 %collective-permute-start.4 = (f32[2,64,256]{1,0,2:T(2,128)S(1)}, f32[2,64,256]{1,0,2:T(2,128)S(1)}, u32[]{:S(2)}, u32[]{:S(2)}) collective-permute-start(f32[2,64,256]{1,0,2:T(2,128)S(1)} %get-tuple-element.14), channel_id=1, source_target_pairs={{0,16},{1,17},{2,18},{3,19},{4,20},{5,21},{6,22},{7,23},{8,24},{9,... | collective-permute-start | bytes 393224 | tf_op jit(solution)/shard_map/ppermute | solution.py:21
  29.3 7.0 %collective-permute-start.3 = (f32[2,128,256]{1,0,2:T(2,128)}, f32[2,128,256]{1,0,2:T(2,128)S(1)}, u32[]{:S(2)}, u32[]{:S(2)}) collective-permute-start(f32[2,128,256]{1,0,2:T(2,128)} %get-tuple-element.15), channel_id=1, source_target_pairs={{4,0},{5,1},{6,2},{7,3},{8,4},{9,5},{10,6},{11,7},{12,8},{13,9},{1... | collective-permute-start | bytes 786440 | tf_op jit(solution)/shard_map/ppermute | solution.py:21
  38.2 3.6 %collective-permute-start.1 = (f32[2,128,256]{1,0,2:T(2,128)S(1)}, f32[2,128,256]{1,0,2:T(2,128)S(1)}, u32[]{:S(2)}, u32[]{:S(2)}) collective-permute-start(f32[2,128,256]{1,0,2:T(2,128)S(1)} %get-tuple-element.17), channel_id=1, source_target_pairs={{1,0},{2,1},{3,2},{4,3},{5,4},{6,5},{7,6},{8,7},{9,8},{10,9},{11,1... | collective-permute-start | bytes 786440 | tf_op jit(solution)/shard_map/ppermute | solution.py:21
  45.5 7.2 %collective-permute-done.2 = f32[2,128,256]{1,0,2:T(2,128)S(1)} collective-permute-done((f32[2,128,256]{1,0,2:T(2,128)}, f32[2,128,256]{1,0,2:T(2,128)S(1)}, u32[]{:S(2)}, u32[]{:S(2)}) %collective-permute-start.2) | collective-permute-done | bytes 262176 | tf_op jit(solution)/shard_map/ppermute | solution.py:21
  52.9 3.4 %collective-permute-done = f32[2,128,256]{1,0,2:T(2,128)S(1)} collective-permute-done((f32[2,128,256]{1,0,2:T(2,128)S(1)}, f32[2,128,256]{1,0,2:T(2,128)S(1)}, u32[]{:S(2)}, u32[]{:S(2)}) %collective-permute-start) | collective-permute-done | bytes 262176 | tf_op jit(solution)/shard_map/ppermute | solution.py:21
  56.4 4.9 %concatenate.92 = f32[2,640,256]{1,0,2:T(2,128)S(1)} concatenate(f32[2,128,256]{1,0,2:T(2,128)S(1)} %broadcast_select_fusion.12, f32[2,128,256]{1,0,2:T(2,128)S(1)} %broadcast_select_fusion.10, f32[2,128,256]{1,0,2:T(2,128)S(1)} %broadcast_select_fusion.8, f32[2,128,256]{1,0,2:T(2,128)S(1)} %broadcast_select_fusion.6, f32[2,64,256]{1,0,2:T(2,128)S(1)} %broadcast_select_fusion.4, ...), dimensions={1} | concatenate | bytes 2621440 | tf_op jit(solution)/shard_map/concatenate | solution.py:78
  61.4 8.5 %fusion.19 = f32[1280,256]{0,1:T(8,128)S(1)} fusion(f32[1280,256]{0,1:T(8,128)S(1)} %bitcast.60, f32[1,1,1280,1280]{3,2,1,0:T(8,128)} %param.4, pred[256]{0:T(512)(128)(4,1)S(1)} %get-tuple-element.31, bf16[256,1280]{1,0:T(8,128)(2,1)S(1)} %gather_fusion, pred[256]{0:T(512)(128)(4,1)S(1)} %get-tuple-element.5), kind=kOutput, calls=%fused_computation.14 | convolution fusion | flops 5034475520 | bytes 9830912 | tf_op jit(solution)/shard_map/dot_general | solution.py:104
  72.9 3.4 %collective-permute-start.10 = (f32[2,64,256]{1,0,2:T(2,128)S(1)}, f32[2,64,256]{1,0,2:T(2,128)S(1)}, u32[]{:S(2)}, u32[]{:S(2)}) collective-permute-start(f32[2,64,256]{1,0,2:T(2,128)S(1)} %get-tuple-element.8), channel_id=1, source_target_pairs={{0,16},{1,17},{2,18},{3,19},{4,20},{5,21},{6,22},{7,23},{8,24},{9,... | collective-permute-start | bytes 393224 | tf_op jit(solution)/shard_map/ppermute | solution.py:21
  76.6 6.3 %collective-permute-start.9 = (f32[2,128,256]{1,0,2:T(2,128)S(1)}, f32[2,128,256]{1,0,2:T(2,128)S(1)}, u32[]{:S(2)}, u32[]{:S(2)}) collective-permute-start(f32[2,128,256]{1,0,2:T(2,128)S(1)} %get-tuple-element.9), channel_id=1, source_target_pairs={{4,0},{5,1},{6,2},{7,3},{8,4},{9,5},{10,6},{11,7},{12,8},{13,9},{1... | collective-permute-start | bytes 786440 | tf_op jit(solution)/shard_map/ppermute | solution.py:21
  84.8 4.2 %collective-permute-start.7 = (f32[2,128,256]{1,0,2:T(2,128)S(1)}, f32[2,128,256]{1,0,2:T(2,128)S(1)}, u32[]{:S(2)}, u32[]{:S(2)}) collective-permute-start(f32[2,128,256]{1,0,2:T(2,128)S(1)} %get-tuple-element.11), channel_id=1, source_target_pairs={{1,0},{2,1},{3,2},{4,3},{5,4},{6,5},{7,6},{8,7},{9,8},{10,9},{11,1... | collective-permute-start | bytes 786440 | tf_op jit(solution)/shard_map/ppermute | solution.py:21
  93.9 4.9 %collective-permute-done.7 = f32[2,128,256]{1,0,2:T(2,128)S(1)} collective-permute-done((f32[2,128,256]{1,0,2:T(2,128)S(1)}, f32[2,128,256]{1,0,2:T(2,128)S(1)}, u32[]{:S(2)}, u32[]{:S(2)}) %collective-permute-start.7) | collective-permute-done | bytes 262176 | tf_op jit(solution)/shard_map/ppermute | solution.py:21
  99.0 4.2 %collective-permute-done.6 = f32[2,128,256]{1,0,2:T(2,128)S(1)} collective-permute-done((f32[2,128,256]{1,0,2:T(2,128)S(1)}, f32[2,128,256]{1,0,2:T(2,128)S(1)}, u32[]{:S(2)}, u32[]{:S(2)}) %collective-permute-start.6) | collective-permute-done | bytes 262176 | tf_op jit(solution)/shard_map/ppermute | solution.py:21
  103.3 4.9 %concatenate.93 = f32[2,640,256]{1,0,2:T(2,128)S(1)} concatenate(f32[2,128,256]{1,0,2:T(2,128)S(1)} %broadcast_select_fusion.11, f32[2,128,256]{1,0,2:T(2,128)S(1)} %broadcast_select_fusion.9, f32[2,128,256]{1,0,2:T(2,128)S(1)} %broadcast_select_fusion.7, f32[2,128,256]{1,0,2:T(2,128)S(1)} %broadcast_select_fusion.5, f32[2,64,256]{1,0,2:T(2,128)S(1)} %broadcast_select_fusion.3, ...), dimensions={1} | concatenate | bytes 2621440 | tf_op jit(solution)/shard_map/concatenate | solution.py:78
  108.3 8.5 %fusion.16 = bf16[1280,256]{0,1:T(8,128)(2,1)S(1)} fusion(f32[1280,256]{0,1:T(8,128)S(1)} %bitcast.59, f32[1,1,1280,1280]{3,2,1,0:T(8,128)} %param.4, pred[256]{0:T(512)(128)(4,1)S(1)} %get-tuple-element.31, bf16[256,1280]{1,0:T(8,128)(2,1)S(1)} %gather_fusion, pred[256]{0:T(512)(128)(4,1)S(1)} %get-tuple-element.5), kind=kOutput, calls=%fused_computation.13 | convolution fusion | flops 5034803200 | bytes 9175552 | tf_op jit(solution)/shard_map/dot_general | solution.py:104
  119.8 3.1 %collective-permute-start.16 = (bf16[2,64,256]{1,0,2:T(2,128)(2,1)S(1)}, bf16[2,64,256]{1,0,2:T(2,128)(2,1)S(1)}, u32[]{:S(2)}, u32[]{:S(2)}) collective-permute-start(bf16[2,64,256]{1,0,2:T(2,128)(2,1)S(1)} %get-tuple-element.26), channel_id=1, source_target_pairs={{0,16},{1,17},{2,18},{3,19},{4,20},{5,21},{6,22},{7,23},{8,24},{9,... | collective-permute-start | bytes 196616 | tf_op jit(solution)/shard_map/ppermute | solution.py:21
  122.9 5.7 %collective-permute-start.15 = (bf16[2,128,256]{1,0,2:T(2,128)(2,1)S(1)}, bf16[2,128,256]{1,0,2:T(2,128)(2,1)S(1)}, u32[]{:S(2)}, u32[]{:S(2)}) collective-permute-start(bf16[2,128,256]{1,0,2:T(2,128)(2,1)S(1)} %get-tuple-element.27), channel_id=1, source_target_pairs={{4,0},{5,1},{6,2},{7,3},{8,4},{9,5},{10,6},{11,7},{12,8},{13,9},{1... | collective-permute-start | bytes 393224 | tf_op jit(solution)/shard_map/ppermute | solution.py:21
  133.3 2.8 %collective-permute-start.12 = (bf16[2,128,256]{1,0,2:T(2,128)(2,1)S(1)}, bf16[2,128,256]{1,0,2:T(2,128)(2,1)S(1)}, u32[]{:S(2)}, u32[]{:S(2)}) collective-permute-start(bf16[2,128,256]{1,0,2:T(2,128)(2,1)S(1)} %get-tuple-element.30), channel_id=1, source_target_pairs={{0,1},{1,2},{2,3},{3,4},{4,5},{5,6},{6,7},{7,8},{8,9},{9,10},{10,1... | collective-permute-start | bytes 393224 | tf_op jit(solution)/shard_map/ppermute | solution.py:21
  136.5 4.3 %collective-permute-done.14 = bf16[2,128,256]{1,0,2:T(2,128)(2,1)S(1)} collective-permute-done((bf16[2,128,256]{1,0,2:T(2,128)(2,1)S(1)}, bf16[2,128,256]{1,0,2:T(2,128)(2,1)S(1)}, u32[]{:S(2)}, u32[]{:S(2)}) %collective-permute-start.14) | collective-permute-done | bytes 131104 | tf_op jit(solution)/shard_map/ppermute | solution.py:21
  141.2 3.9 %concatenate.94 = bf16[2,640,256]{1,0,2:T(2,128)(2,1)S(1)} concatenate(bf16[2,128,256]{1,0,2:T(2,128)(2,1)S(1)} %select_convert_fusion.5, bf16[2,128,256]{1,0,2:T(2,128)(2,1)S(1)} %select_convert_fusion.4, bf16[2,128,256]{1,0,2:T(2,128)(2,1)S(1)} %select_convert_fusion.3, bf16[2,128,256]{1,0,2:T(2,128)(2,1)S(1)} %select_convert_fusion.2, ...), dimensions={1} | concatenate | bytes 1310720 | tf_op jit(solution)/shard_map/concatenate | solution.py:78
  145.2 4.1 %fusion.26 = bf16[2048,256]{0,1:T(8,128)(2,1)S(1)} fusion(bf16[1280,256]{0,1:T(8,128)(2,1)S(1)} %bitcast.65, s32[256]{0:T(256)S(1)} %get-tuple-element.6, pred[256]{0:T(512)(128)(4,1)S(1)} %get-tuple-element.31, bf16[1,1,2048,1280]{3,2,1,0:T(8,128)(2,1)} %param.5), kind=kOutput, calls=%fused_computation.17 | convolution fusion | flops 1345323008 | bytes 6948096 | tf_op jit(solution)/shard_map/dot_general | solution.py:108
  151.6 2.8 %subtract_multiply_fusion = f32[1024,1024]{1,0:T(8,128)} fusion(f32[1024,1024]{1,0:T(8,128)S(1)} %fusion.29, f32[1024,1024]{1,0:T(8,128)S(1)} %fusion.37, f32[1024,1024]{1,0:T(8,128)S(1)} %fusion.36, bf16[1024,128]{0,1:T(8,128)(2,1)S(1)} %get-tuple-element.19, bf16[1024,128]{0,1:T(8,128)(2,1)S(1)} %get-tuple-element.21, ...), kind=kOutput, calls=%fused_computation.7 | convolution fusion | flops 543162368 | bytes 17563648 | tf_op jit(solution)/shard_map/dot_general | solution.py:49
  154.5 61.2 %reduce-scatter.2.cloned.1.call-done = f32[256,1024]{1,0:T(8,128)} async-done(((f32[1024,1024]{1,0:T(8,128)}), f32[256,1024]{1,0:T(8,128)}) %reduce-scatter.2.cloned.1.call-update) | async-done | bytes 1048592 | tf_op jit(solution)/shard_map/reduce_scatter | solution.py:115
  (64 shorter events, 33.4 us)
Async XLA Ops:
  6.5 209.1 %reduce-scatter.2.cloned.1.call-start = ((), (), s32[]{:S(2)}) async-start(), calls=%async_computation.1 | async-start | bytes 5242880 | tf_op jit(solution)/shard_map/reduce_scatter | solution.py:115
  22.9 19.1 %collective-permute-start.5 = (f32[2,64,256]{1,0,2:T(2,128)S(1)}, f32[2,64,256]{1,0,2:T(2,128)S(1)}, u32[]{:S(2)}, u32[]{:S(2)}) collective-permute-start(f32[2,64,256]{1,0,2:T(2,128)S(1)} %get-tuple-element.13), channel_id=1, source_target_pairs={{16,0},{17,1},{18,2},{19,3},{20,4},{21,5},{22,6},{23,7},{24,8},{25... | collective-permute-start | bytes 393224 | tf_op jit(solution)/shard_map/ppermute | solution.py:21
  25.0 19.2 %collective-permute-start.4 = (f32[2,64,256]{1,0,2:T(2,128)S(1)}, f32[2,64,256]{1,0,2:T(2,128)S(1)}, u32[]{:S(2)}, u32[]{:S(2)}) collective-permute-start(f32[2,64,256]{1,0,2:T(2,128)S(1)} %get-tuple-element.14), channel_id=1, source_target_pairs={{0,16},{1,17},{2,18},{3,19},{4,20},{5,21},{6,22},{7,23},{8,24},{9,... | collective-permute-start | bytes 393224 | tf_op jit(solution)/shard_map/ppermute | solution.py:21
  29.3 16.1 %collective-permute-start.3 = (f32[2,128,256]{1,0,2:T(2,128)}, f32[2,128,256]{1,0,2:T(2,128)S(1)}, u32[]{:S(2)}, u32[]{:S(2)}) collective-permute-start(f32[2,128,256]{1,0,2:T(2,128)} %get-tuple-element.15), channel_id=1, source_target_pairs={{4,0},{5,1},{6,2},{7,3},{8,4},{9,5},{10,6},{11,7},{12,8},{13,9},{1... | collective-permute-start | bytes 786440 | tf_op jit(solution)/shard_map/ppermute | solution.py:21
  36.3 16.4 %collective-permute-start.2 = (f32[2,128,256]{1,0,2:T(2,128)}, f32[2,128,256]{1,0,2:T(2,128)S(1)}, u32[]{:S(2)}, u32[]{:S(2)}) collective-permute-start(f32[2,128,256]{1,0,2:T(2,128)} %get-tuple-element.16), channel_id=1, source_target_pairs={{0,4},{1,5},{2,6},{3,7},{4,8},{5,9},{6,10},{7,11},{8,12},{9,13},{1... | collective-permute-start | bytes 786440 | tf_op jit(solution)/shard_map/ppermute | solution.py:21
  38.2 14.5 %collective-permute-start.1 = (f32[2,128,256]{1,0,2:T(2,128)S(1)}, f32[2,128,256]{1,0,2:T(2,128)S(1)}, u32[]{:S(2)}, u32[]{:S(2)}) collective-permute-start(f32[2,128,256]{1,0,2:T(2,128)S(1)} %get-tuple-element.17), channel_id=1, source_target_pairs={{1,0},{2,1},{3,2},{4,3},{5,4},{6,5},{7,6},{8,7},{9,8},{10,9},{11,1... | collective-permute-start | bytes 786440 | tf_op jit(solution)/shard_map/ppermute | solution.py:21
  42.0 14.3 %collective-permute-start = (f32[2,128,256]{1,0,2:T(2,128)S(1)}, f32[2,128,256]{1,0,2:T(2,128)S(1)}, u32[]{:S(2)}, u32[]{:S(2)}) collective-permute-start(f32[2,128,256]{1,0,2:T(2,128)S(1)} %get-tuple-element.18), channel_id=1, source_target_pairs={{0,1},{1,2},{2,3},{3,4},{4,5},{5,6},{6,7},{7,8},{8,9},{9,10},{10,1... | collective-permute-start | bytes 786440 | tf_op jit(solution)/shard_map/ppermute | solution.py:21
  71.0 18.0 %collective-permute-start.11 = (f32[2,64,256]{1,0,2:T(2,128)S(1)}, f32[2,64,256]{1,0,2:T(2,128)S(1)}, u32[]{:S(2)}, u32[]{:S(2)}) collective-permute-start(f32[2,64,256]{1,0,2:T(2,128)S(1)} %get-tuple-element.7), channel_id=1, source_target_pairs={{16,0},{17,1},{18,2},{19,3},{20,4},{21,5},{22,6},{23,7},{24,8},{25... | collective-permute-start | bytes 393224 | tf_op jit(solution)/shard_map/ppermute | solution.py:21
  72.9 18.4 %collective-permute-start.10 = (f32[2,64,256]{1,0,2:T(2,128)S(1)}, f32[2,64,256]{1,0,2:T(2,128)S(1)}, u32[]{:S(2)}, u32[]{:S(2)}) collective-permute-start(f32[2,64,256]{1,0,2:T(2,128)S(1)} %get-tuple-element.8), channel_id=1, source_target_pairs={{0,16},{1,17},{2,18},{3,19},{4,20},{5,21},{6,22},{7,23},{8,24},{9,... | collective-permute-start | bytes 393224 | tf_op jit(solution)/shard_map/ppermute | solution.py:21
  76.6 14.8 %collective-permute-start.9 = (f32[2,128,256]{1,0,2:T(2,128)S(1)}, f32[2,128,256]{1,0,2:T(2,128)S(1)}, u32[]{:S(2)}, u32[]{:S(2)}) collective-permute-start(f32[2,128,256]{1,0,2:T(2,128)S(1)} %get-tuple-element.9), channel_id=1, source_target_pairs={{4,0},{5,1},{6,2},{7,3},{8,4},{9,5},{10,6},{11,7},{12,8},{13,9},{1... | collective-permute-start | bytes 786440 | tf_op jit(solution)/shard_map/ppermute | solution.py:21
  82.9 10.9 %collective-permute-start.8 = (f32[2,128,256]{1,0,2:T(2,128)S(1)}, f32[2,128,256]{1,0,2:T(2,128)S(1)}, u32[]{:S(2)}, u32[]{:S(2)}) collective-permute-start(f32[2,128,256]{1,0,2:T(2,128)S(1)} %get-tuple-element.10), channel_id=1, source_target_pairs={{0,4},{1,5},{2,6},{3,7},{4,8},{5,9},{6,10},{7,11},{8,12},{9,13},{1... | collective-permute-start | bytes 786440 | tf_op jit(solution)/shard_map/ppermute | solution.py:21
  84.8 14.0 %collective-permute-start.7 = (f32[2,128,256]{1,0,2:T(2,128)S(1)}, f32[2,128,256]{1,0,2:T(2,128)S(1)}, u32[]{:S(2)}, u32[]{:S(2)}) collective-permute-start(f32[2,128,256]{1,0,2:T(2,128)S(1)} %get-tuple-element.11), channel_id=1, source_target_pairs={{1,0},{2,1},{3,2},{4,3},{5,4},{6,5},{7,6},{8,7},{9,8},{10,9},{11,1... | collective-permute-start | bytes 786440 | tf_op jit(solution)/shard_map/ppermute | solution.py:21
  89.0 14.2 %collective-permute-start.6 = (f32[2,128,256]{1,0,2:T(2,128)S(1)}, f32[2,128,256]{1,0,2:T(2,128)S(1)}, u32[]{:S(2)}, u32[]{:S(2)}) collective-permute-start(f32[2,128,256]{1,0,2:T(2,128)S(1)} %get-tuple-element.12), channel_id=1, source_target_pairs={{0,1},{1,2},{2,3},{3,4},{4,5},{5,6},{6,7},{7,8},{8,9},{9,10},{10,1... | collective-permute-start | bytes 786440 | tf_op jit(solution)/shard_map/ppermute | solution.py:21
  117.2 16.1 %collective-permute-start.17 = (bf16[2,64,256]{1,0,2:T(2,128)(2,1)S(1)}, bf16[2,64,256]{1,0,2:T(2,128)(2,1)S(1)}, u32[]{:S(2)}, u32[]{:S(2)}) collective-permute-start(bf16[2,64,256]{1,0,2:T(2,128)(2,1)S(1)} %get-tuple-element.25), channel_id=1, source_target_pairs={{16,0},{17,1},{18,2},{19,3},{20,4},{21,5},{22,6},{23,7},{24,8},{25... | collective-permute-start | bytes 196616 | tf_op jit(solution)/shard_map/ppermute | solution.py:21
  119.8 16.5 %collective-permute-start.16 = (bf16[2,64,256]{1,0,2:T(2,128)(2,1)S(1)}, bf16[2,64,256]{1,0,2:T(2,128)(2,1)S(1)}, u32[]{:S(2)}, u32[]{:S(2)}) collective-permute-start(bf16[2,64,256]{1,0,2:T(2,128)(2,1)S(1)} %get-tuple-element.26), channel_id=1, source_target_pairs={{0,16},{1,17},{2,18},{3,19},{4,20},{5,21},{6,22},{7,23},{8,24},{9,... | collective-permute-start | bytes 196616 | tf_op jit(solution)/shard_map/ppermute | solution.py:21
  122.9 13.5 %collective-permute-start.15 = (bf16[2,128,256]{1,0,2:T(2,128)(2,1)S(1)}, bf16[2,128,256]{1,0,2:T(2,128)(2,1)S(1)}, u32[]{:S(2)}, u32[]{:S(2)}) collective-permute-start(bf16[2,128,256]{1,0,2:T(2,128)(2,1)S(1)} %get-tuple-element.27), channel_id=1, source_target_pairs={{4,0},{5,1},{6,2},{7,3},{8,4},{9,5},{10,6},{11,7},{12,8},{13,9},{1... | collective-permute-start | bytes 393224 | tf_op jit(solution)/shard_map/ppermute | solution.py:21
  128.7 12.2 %collective-permute-start.14 = (bf16[2,128,256]{1,0,2:T(2,128)(2,1)S(1)}, bf16[2,128,256]{1,0,2:T(2,128)(2,1)S(1)}, u32[]{:S(2)}, u32[]{:S(2)}) collective-permute-start(bf16[2,128,256]{1,0,2:T(2,128)(2,1)S(1)} %get-tuple-element.28), channel_id=1, source_target_pairs={{0,4},{1,5},{2,6},{3,7},{4,8},{5,9},{6,10},{7,11},{8,12},{9,13},{1... | collective-permute-start | bytes 393224 | tf_op jit(solution)/shard_map/ppermute | solution.py:21
  130.6 10.3 %collective-permute-start.13 = (bf16[2,128,256]{1,0,2:T(2,128)(2,1)S(1)}, bf16[2,128,256]{1,0,2:T(2,128)(2,1)S(1)}, u32[]{:S(2)}, u32[]{:S(2)}) collective-permute-start(bf16[2,128,256]{1,0,2:T(2,128)(2,1)S(1)} %get-tuple-element.29), channel_id=1, source_target_pairs={{1,0},{2,1},{3,2},{4,3},{5,4},{6,5},{7,6},{8,7},{9,8},{10,9},{11,1... | collective-permute-start | bytes 393224 | tf_op jit(solution)/shard_map/ppermute | solution.py:21
  133.3 7.7 %collective-permute-start.12 = (bf16[2,128,256]{1,0,2:T(2,128)(2,1)S(1)}, bf16[2,128,256]{1,0,2:T(2,128)(2,1)S(1)}, u32[]{:S(2)}, u32[]{:S(2)}) collective-permute-start(bf16[2,128,256]{1,0,2:T(2,128)(2,1)S(1)} %get-tuple-element.30), channel_id=1, source_target_pairs={{0,1},{1,2},{2,3},{3,4},{4,5},{5,6},{6,7},{7,8},{8,9},{9,10},{10,1... | collective-permute-start | bytes 393224 | tf_op jit(solution)/shard_map/ppermute | solution.py:21
Sparse Core Ops, SparseCore 0:
  154.6 61.0 reduce-scatter.1
where the time goes:
time: 224 us; the launch traced here: 222 us
  waiting for transfers between devices  88.5 us (40%)
  starting transfers between devices  58.2 us (26%)
  matrix products  34.5 us (15%)
  local copies, waits for them, and re-layouts  24.5 us (11%)
  between operations  14 us (6%)
  other arithmetic  2.88 us (1%)
    reduce_scatter x1, waiting for transfers between devices, local(): lax.psum_scatter(hessian_terms(fields), 'freq', scatter_dimension=0, tile...  61.2 us
    ppermute x18, starting transfers between devices, shifted(): return lax.ppermute(value, axis, pairs)  58.2 us
    ppermute x18, waiting for transfers between devices, shifted(): return lax.ppermute(value, axis, pairs)  27.3 us
    dot_general x3, matrix products, local(): jnp.dot(operator, incoming_trace_values, precision=lax.Precision.HIGHEST)  25.3 us
    concatenate x3, local copies, waits for them, and re-layouts, swap_faces(): return jnp.concatenate(pieces, axis=1).reshape(TRACE, RHS)  13.6 us
    gather x1, local copies, waits for them, and re-layouts, local(): picked = jnp.take(interior, local_cell, axis=0).astype(jnp.float32)  4.94 us
  transfers between devices with their start and end apart: 19, of which 8 were waited for; matrix products, arithmetic and copies ran while one was open for 2% of the time, Pallas kernels for 0%

commit v1 on v0

v1 whole, which is shorter than its diff:
```python
import jax
import jax.numpy as jnp
from jax import lax
from jax.experimental import pallas as pl
from jax.experimental.pallas import tpu as pltpu
from jax.sharding import PartitionSpec as P

CX = 8
CY = 8
CZ = 16
NSRC = 128
NRCV = 128
SWEEPS = 3
CELLS = 1024
FACES = 640
TRACE = 1280
RHS = 256
ROWS = 256
BLOCKS = CELLS // ROWS
MESH = pl.DeviceIdType.MESH
COUNTS = (CY * CZ, CY * CZ, CX * CZ, CX * CZ, CX * CY, CX * CY)
BEGINS = tuple(sum(COUNTS[:i]) for i in range(6))
PARTNER = (1, 0, 3, 2, 5, 4)
ORDER = (2, 3, 0, 1, 4, 5)
NT = (((1,), (1,)), ((), ()))


def kernel(
    nsub,
    cells_row,
    cells_col,
    z_hbm,
    interior_hbm,
    out_ref,
    zf,
    zb,
    interior,
    inc,
    outb,
    lu,
    ru,
    lv,
    rv,
    send_a,
    recv_a,
    send_y,
    recv_y,
    load_sem,
    face_send,
    face_recv,
    a_send,
    a_recv,
    y_send,
    y_recv,
):
    sub = lax.axis_index("sub")
    freq = lax.axis_index("freq")
    grid_x = min(4, nsub)
    grid_y = min(4, nsub // grid_x)
    grid_z = nsub // (grid_x * grid_y)
    sizes = (grid_x, grid_y, grid_z)
    strides = (1, grid_x, grid_x * grid_y)
    coords = (sub % grid_x, sub // grid_x % grid_y, sub // (grid_x * grid_y))
    valid = []
    beside = []
    for face in range(6):
        axis = face // 2
        if face % 2 == 0:
            valid.append(coords[axis] > 0)
            beside.append(sub - strides[axis])
        else:
            valid.append(coords[axis] < sizes[axis] - 1)
            beside.append(sub + strides[axis])
    chip = freq // 2
    core = freq % 2
    sibling = {"freq": chip * 2 + 1 - core}
    across = {"freq": (1 - chip) * 2 + core}

    def fetch(part):
        rows = pl.ds(part * CELLS, CELLS)
        return pltpu.make_async_copy(interior_hbm.at[rows], interior.at[rows], load_sem.at[part])

    fetch_z = pltpu.make_async_copy(z_hbm, zf, load_sem.at[2])
    fetch(0).start()
    fetch_z.start()
    fetch(1).start()

    barrier = pltpu.get_barrier_semaphore()
    greeted = jnp.int32(2)
    for face in range(6):
        greeted = greeted + valid[face].astype(jnp.int32)

        @pl.when(valid[face])
        def _():
            pl.semaphore_signal(barrier, inc=1, device_id={"sub": beside[face]}, device_id_type=MESH)

    pl.semaphore_signal(barrier, inc=1, device_id=sibling, device_id_type=MESH)
    pl.semaphore_signal(barrier, inc=1, device_id=across, device_id_type=MESH)

    def span(face):
        return pl.ds(BEGINS[face], COUNTS[face])

    for face in range(6):

        @pl.when(jnp.logical_not(valid[face]))
        def _():
            for k in range(SWEEPS):
                inc[k, :, span(face), :] = jnp.zeros((2, COUNTS[face], RHS), jnp.bfloat16)

    def outward(k, face):
        other = PARTNER[face]
        return pltpu.make_async_remote_copy(
            src_ref=outb.at[k, :, span(face), :],
            dst_ref=inc.at[k, :, span(other), :],
            send_sem=face_send.at[k, face],
            recv_sem=face_recv.at[k, other],
            device_id={"sub": beside[face]},
            device_id_type=MESH,
        )

    def inward(k, face):
        return pltpu.make_async_remote_copy(
            src_ref=outb.at[k, :, span(face), :],
            dst_ref=inc.at[k, :, span(face), :],
            send_sem=face_send.at[k, face],
            recv_sem=face_recv.at[k, face],
            device_id={"sub": beside[face]},
            device_id_type=MESH,
        )

    def send(k, face):
        @pl.when(valid[face])
        def _():
            outward(k, face).start()

    def receive(k):
        for face in ORDER:

            @pl.when(valid[face])
            def _():
                inward(k, face).wait_recv()

    first = sub * CELLS
    hot = cells_col[...] == first + lax.broadcasted_iota(jnp.int32, (RHS, CELLS), 1)
    hot = hot.astype(jnp.float32).astype(jnp.bfloat16)
    fetch(0).wait()
    picked = jnp.dot(hot, interior[:CELLS, :], preferred_element_type=jnp.float32)
    load = picked.T.astype(jnp.bfloat16)
    outb[0, 0] = load[:FACES]
    outb[0, 1] = load[FACES:]
    pl.semaphore_wait(barrier, greeted)
    for face in ORDER:
        send(0, face)

    fetch_z.wait()

    @pl.loop(0, TRACE // 128)
    def _(i):
        rows = pl.ds(pl.multiple_of(i * 128, 128), 128)
        zb[rows, :] = zf[rows, :].astype(jnp.bfloat16)

    for k in range(1, SWEEPS):
        receive(k - 1)
        arrived = inc[k - 1].reshape(TRACE, RHS)
        for face in ORDER[::2]:
            begin = BEGINS[face]
            count = COUNTS[face] * 2
            z_rows = jnp.concatenate([zb[begin : begin + count, :], zb[FACES + begin : FACES + begin + count, :]], axis=0)
            product = jnp.dot(z_rows, arrived, preferred_element_type=jnp.float32)
            for part in range(2):
                added = outb[0, part, begin : begin + count, :].astype(jnp.float32)
                total = product[part * count : (part + 1) * count] + added
                outb[k, part, begin : begin + count, :] = total.astype(jnp.bfloat16)
            send(k, face)
            send(k, face + 1)
    fetch(1).wait()
    receive(SWEEPS - 1)

    field_scale = jnp.float32(TRACE ** (-0.5))

    @pl.loop(0, BLOCKS)
    def _(i):
        begin = pl.multiple_of(i * ROWS, ROWS)
        trace = inc[SWEEPS - 1].reshape(TRACE, RHS)
        rows = pl.ds(begin, ROWS)
        real = jnp.dot(interior[rows, :], trace, preferred_element_type=jnp.float32)
        low = pl.ds(pl.multiple_of(CELLS + i * ROWS, ROWS), ROWS)
        imag = jnp.dot(interior[low, :], trace, preferred_element_type=jnp.float32)
        point = cells_row[...] == first + begin + lax.broadcasted_iota(jnp.int32, (ROWS, RHS), 0)
        real = real * field_scale + point.astype(jnp.float32)
        imag = imag * field_scale
        real_b = real.astype(jnp.bfloat16)
        imag_b = imag.astype(jnp.bfloat16)
        minus_b = (-real).astype(jnp.bfloat16)
        lu[rows, :NSRC] = real_b[:, :NSRC]
        lu[rows, NSRC:] = imag_b[:, :NSRC]
        ru[rows, :NSRC] = imag_b[:, :NSRC]
        ru[rows, NSRC:] = minus_b[:, :NSRC]
        lv[rows, :NRCV] = real_b[:, NSRC:]
        lv[rows, NRCV:] = imag_b[:, NSRC:]
        rv[rows, :NRCV] = imag_b[:, NSRC:]
        rv[rows, NRCV:] = minus_b[:, NSRC:]

    def term(owner, j):
        rows = pl.ds(pl.multiple_of(owner * ROWS, ROWS), ROWS)
        cols = pl.ds(pl.multiple_of(j * ROWS, ROWS), ROWS)
        left_u = jnp.concatenate([lu[rows, :], ru[rows, :]], axis=0)
        gram_u = lax.dot_general(left_u, lu[cols, :], NT, preferred_element_type=jnp.float32)
        left_v = jnp.concatenate([lv[rows, :], rv[rows, :]], axis=0)
        gram_v = lax.dot_general(left_v, lv[cols, :], NT, preferred_element_type=jnp.float32)
        both = gram_u * gram_v
        return (both[:ROWS] - both[ROWS:]) * jnp.float32(1.0 / (NSRC * NRCV))

    def to_sibling(half, j):
        return pltpu.make_async_remote_copy(
            src_ref=send_a.at[half, j],
            dst_ref=recv_a.at[half, j],
            send_sem=a_send.at[half, j],
            recv_sem=a_recv.at[half, j],
            device_id=sibling,
            device_id_type=MESH,
        )

    def to_across(j):
        return pltpu.make_async_remote_copy(
            src_ref=send_y.at[j],
            dst_ref=recv_y.at[j],
            send_sem=y_send.at[j],
            recv_sem=y_recv.at[j],
            device_id=across,
            device_id_type=MESH,
        )

    @pl.loop(0, BLOCKS)
    def _(j):
        send_a[0, j] = term((1 - chip) * 2 + 1 - core, j).astype(jnp.bfloat16)
        to_sibling(0, j).start()

    @pl.loop(0, BLOCKS)
    def _(j):
        own = term((1 - chip) * 2 + core, j)
        to_sibling(0, j).wait_recv()
        send_y[j] = (own + recv_a[0, j].astype(jnp.float32)).astype(jnp.bfloat16)
        to_across(j).start()

    @pl.loop(0, BLOCKS)
    def _(j):
        send_a[1, j] = term(chip * 2 + 1 - core, j).astype(jnp.bfloat16)
        to_sibling(1, j).start()

    @pl.loop(0, BLOCKS)
    def _(j):
        own = term(chip * 2 + core, j)
        to_sibling(1, j).wait_recv()
        cols = pl.ds(pl.multiple_of(j * ROWS, ROWS), ROWS)
        out_ref[:, cols] = own + recv_a[1, j].astype(jnp.float32)

    @pl.loop(0, BLOCKS)
    def _(j):
        to_across(j).wait_recv()
        cols = pl.ds(pl.multiple_of(j * ROWS, ROWS), ROWS)
        out_ref[:, cols] = out_ref[:, cols] + recv_y[j].astype(jnp.float32)

    for k in range(SWEEPS):
        for face in range(6):

            @pl.when(valid[face])
            def _():
                outward(k, face).wait_send()

    @pl.loop(0, BLOCKS)
    def _(j):
        to_sibling(0, j).wait_send()
        to_sibling(1, j).wait_send()
        to_across(j).wait_send()


def local(impedance, interior_map, source_cells, receiver_cells):
    nsub = lax.axis_size("sub")
    cells = jnp.concatenate([source_cells, receiver_cells])
    bf16 = jnp.bfloat16
    vmem = pl.BlockSpec(memory_space=pltpu.VMEM)
    anywhere = pl.BlockSpec(memory_space=pl.ANY)

    def body(*refs):
        kernel(nsub, *refs)

    owned = pl.pallas_call(
        body,
        name="schwarz_hessian",
        out_shape=jax.ShapeDtypeStruct((ROWS, CELLS), jnp.float32),
        in_specs=[vmem, vmem, anywhere, anywhere],
        out_specs=vmem,
        scratch_shapes=[
            pltpu.VMEM((TRACE, TRACE), jnp.float32),
            pltpu.VMEM((TRACE, TRACE), bf16),
            pltpu.VMEM((2 * CELLS, TRACE), bf16),
            pltpu.VMEM((SWEEPS, 2, FACES, RHS), bf16),
            pltpu.VMEM((SWEEPS, 2, FACES, RHS), bf16),
            pltpu.VMEM((CELLS, RHS), bf16),
            pltpu.VMEM((CELLS, RHS), bf16),
            pltpu.VMEM((CELLS, RHS), bf16),
            pltpu.VMEM((CELLS, RHS), bf16),
            pltpu.VMEM((2, BLOCKS, ROWS, ROWS), bf16),
            pltpu.VMEM((2, BLOCKS, ROWS, ROWS), bf16),
            pltpu.VMEM((BLOCKS, ROWS, ROWS), bf16),
            pltpu.VMEM((BLOCKS, ROWS, ROWS), bf16),
            pltpu.SemaphoreType.DMA((3,)),
            pltpu.SemaphoreType.DMA((SWEEPS, 6)),
            pltpu.SemaphoreType.DMA((SWEEPS, 6)),
            pltpu.SemaphoreType.DMA((2, BLOCKS)),
            pltpu.SemaphoreType.DMA((2, BLOCKS)),
            pltpu.SemaphoreType.DMA((BLOCKS,)),
            pltpu.SemaphoreType.DMA((BLOCKS,)),
        ],
        compiler_params=pltpu.CompilerParams(
            collective_id=0, has_side_effects=True, vmem_limit_bytes=60 * 1024 * 1024
        ),
    )(cells[None, :], cells[:, None], impedance[0, 0], interior_map[0, 0])
    return owned[None]


def solution(mesh):
    in_specs = (P("freq", "sub", None, None), P("freq", "sub", None, None), P(), P())
    out_specs = P("sub", "freq", None)
    return jax.shard_map(local, mesh=mesh, in_specs=in_specs, out_specs=out_specs, check_vma=False)
```

time: 224 us -> 63.2 us (0.28)
  the two profiles are of different devices: /device:TPU:35 before, /device:TPU:164 now
where the time goes in v1:
time: 63.2 us; the launch traced here: 63 us
  Pallas kernels  58.5 us (93%)
  local copies, waits for them, and re-layouts  4.44 us (7%)
    pallas_call x1, Pallas kernels, local(): pl.pallas_call(body, name='schwarz_hessian', out_shape=jax.ShapeDtypeStru...  58.5 us
    unnamed x4, local copies, waits for them, and re-layouts  2.98 us

profile of v1, /device:TPU:164, one launch (start us, length us, event | category | flops | bytes accessed | tf_op | source)
XLA Modules:
  0.0 63.0 jit_solution(899098484743076913)
XLA Ops:
  0.0 0.7 %constant_dynamic-update-slice_fusion.1 = s32[256]{0:T(256)S(1)} fusion(s32[256]{0:T(256)S(1)} %custom-call, s32[128]{0:T(128)} %param.6), kind=kLoop, calls=%fused_computation.1 | loop fusion | bytes 1024
  0.7 0.7 %constant_dynamic-update-slice_fusion = s32[256]{0:T(256)S(1)} fusion(s32[256]{0:T(256)S(1)} %constant_dynamic-update-slice_fusion.1, s32[128]{0:T(128)} %param.7), kind=kLoop, calls=%fused_computation | loop fusion | bytes 1024 | tf_op jit(solution)/shard_map/concatenate | solution.py:280
  1.3 0.0 copy-start
  1.3 0.8 %copy.5.refs_1_ = s32[256,1]{1,0:T(8,128)} copy(s32[256,1]{0,1:T(1,128)S(1)} %bitcast.8) | data formatting | bytes 2048 | tf_op jit(solution)/shard_map/broadcast_in_dim | solution.py:319
  2.1 0.0 copy-done
  2.1 58.5 %schwarz_hessian.1 = f32[256,1024]{1,0:T(8,128)} custom-call(s32[1,256]{1,0:T(1,128)} %bitcast.9, s32[256,1]{1,0:T(8,128)} %copy.5.refs_1_, f32[1280,1280]{1,0:T(8,128)} %bitcast.5, bf16[2048,1280]{1,0:T(8,128)(2,1)} %bitcast.6), custom_call_target="tpu_custom_call" | custom-call | tf_op jit(solution)/shard_map/schwarz_hessian/pallas_call | solution.py:288
  60.7 2.3 %copy.9 = f32[1,256,1024]{2,1,0:T(8,128)} copy(f32[1,256,1024]{2,1,0:T(8,128)} %bitcast.7) | data formatting | bytes 2097152
  (1 shorter events, 0.0 us)
Async XLA Ops:
  1.3 0.8 %copy-start = (s32[256]{0:T(256)}, s32[256]{0:T(256)S(1)}, u32[]{:S(2)}) copy-start(s32[256]{0:T(256)S(1)} %constant_dynamic-update-slice_fusion) | copy-start | bytes 3076

commit v2 on v1

--- a/solution.py
+++ b/solution.py
@@ -27,8 +27,8 @@
 
 def kernel(
     nsub,
-    cells_row,
-    cells_col,
+    source_cells,
+    receiver_cells,
     z_hbm,
     interior_hbm,
     out_ref,
@@ -105,52 +105,56 @@
         @pl.when(jnp.logical_not(valid[face]))
         def _():
             for k in range(SWEEPS):
-                inc[k, :, span(face), :] = jnp.zeros((2, COUNTS[face], RHS), jnp.bfloat16)
-
-    def outward(k, face):
+                inc[k, :, :, span(face), :] = jnp.zeros((2, 2, COUNTS[face], NSRC), jnp.bfloat16)
+
+    def outward(k, half, face):
         other = PARTNER[face]
         return pltpu.make_async_remote_copy(
-            src_ref=outb.at[k, :, span(face), :],
-            dst_ref=inc.at[k, :, span(other), :],
-            send_sem=face_send.at[k, face],
-            recv_sem=face_recv.at[k, other],
+            src_ref=outb.at[k, half, :, span(face), :],
+            dst_ref=inc.at[k, half, :, span(other), :],
+            send_sem=face_send.at[k, half, face],
+            recv_sem=face_recv.at[k, half, other],
             device_id={"sub": beside[face]},
             device_id_type=MESH,
         )
 
-    def inward(k, face):
+    def inward(k, half, face):
         return pltpu.make_async_remote_copy(
-            src_ref=outb.at[k, :, span(face), :],
-            dst_ref=inc.at[k, :, span(face), :],
-            send_sem=face_send.at[k, face],
-            recv_sem=face_recv.at[k, face],
+            src_ref=outb.at[k, half, :, span(face), :],
+            dst_ref=inc.at[k, half, :, span(face), :],
+            send_sem=face_send.at[k, half, face],
+            recv_sem=face_recv.at[k, half, face],
             device_id={"sub": beside[face]},
             device_id_type=MESH,
         )
 
-    def send(k, face):
+    def send(k, half, face):
         @pl.when(valid[face])
         def _():
-            outward(k, face).start()
-
-    def receive(k):
+            outward(k, half, face).start()
+
+    def receive(k, half):
         for face in ORDER:
 
             @pl.when(valid[face])
             def _():
-                inward(k, face).wait_recv()
+                inward(k, half, face).wait_recv()
 
     first = sub * CELLS
-    hot = cells_col[...] == first + lax.broadcasted_iota(jnp.int32, (RHS, CELLS), 1)
-    hot = hot.astype(jnp.float32).astype(jnp.bfloat16)
-    fetch(0).wait()
-    picked = jnp.dot(hot, interior[:CELLS, :], preferred_element_type=jnp.float32)
-    load = picked.T.astype(jnp.bfloat16)
-    outb[0, 0] = load[:FACES]
-    outb[0, 1] = load[FACES:]
-    pl.semaphore_wait(barrier, greeted)
-    for face in ORDER:
-        send(0, face)
+    for half, cells in enumerate((source_cells, receiver_cells)):
+        column = jnp.broadcast_to(cells[...] - first, (NSRC, NSRC)).T
+        lanes = lax.broadcasted_iota(jnp.int32, (NSRC, NSRC), 1)
+        hot = jnp.concatenate([(column == lanes + i * NSRC).astype(jnp.float32) for i in range(CELLS // NSRC)], axis=1)
+        if half == 0:
+            fetch(0).wait()
+        picked = jnp.dot(hot.astype(jnp.bfloat16), interior[:CELLS, :], preferred_element_type=jnp.float32)
+        load = picked.T.astype(jnp.bfloat16)
+        outb[0, half, 0] = load[:FACES]
+        outb[0, half, 1] = load[FACES:]
+        if half == 0:
+            pl.semaphore_wait(barrier, greeted)
+        for face in ORDER:
+            send(0, half, face)
 
     fetch_z.wait()
 
@@ -160,46 +164,44 @@
         zb[rows, :] = zf[rows, :].astype(jnp.bfloat16)
 
     for k in range(1, SWEEPS):
-        receive(k - 1)
-        arrived = inc[k - 1].reshape(TRACE, RHS)
-        for face in ORDER[::2]:
-            begin = BEGINS[face]
-            count = COUNTS[face] * 2
-            z_rows = jnp.concatenate([zb[begin : begin + count, :], zb[FACES + begin : FACES + begin + count, :]], axis=0)
-            product = jnp.dot(z_rows, arrived, preferred_element_type=jnp.float32)
-            for part in range(2):
-                added = outb[0, part, begin : begin + count, :].astype(jnp.float32)
-                total = product[part * count : (part + 1) * count] + added
-                outb[k, part, begin : begin + count, :] = total.astype(jnp.bfloat16)
-            send(k, face)
-            send(k, face + 1)
+        for half in range(2):
+            receive(k - 1, half)
+            arrived = inc[k - 1, half].reshape(TRACE, NSRC)
+            for face in ORDER[::2]:
+                begin = BEGINS[face]
+                count = COUNTS[face] * 2
+                z_rows = jnp.concatenate(
+                    [zb[begin : begin + count, :], zb[FACES + begin : FACES + begin + count, :]], axis=0
+                )
+                product = jnp.dot(z_rows, arrived, preferred_element_type=jnp.float32)
+                for part in range(2):
+                    added = outb[0, half, part, begin : begin + count, :].astype(jnp.float32)
+                    total = product[part * count : (part + 1) * count] + added
+                    outb[k, half, part, begin : begin + count, :] = total.astype(jnp.bfloat16)
+                send(k, half, face)
+                send(k, half, face + 1)
     fetch(1).wait()
-    receive(SWEEPS - 1)
 
     field_scale = jnp.float32(TRACE ** (-0.5))
 
-    @pl.loop(0, BLOCKS)
-    def _(i):
-        begin = pl.multiple_of(i * ROWS, ROWS)
-        trace = inc[SWEEPS - 1].reshape(TRACE, RHS)
-        rows = pl.ds(begin, ROWS)
-        real = jnp.dot(interior[rows, :], trace, preferred_element_type=jnp.float32)
-        low = pl.ds(pl.multiple_of(CELLS + i * ROWS, ROWS), ROWS)
-        imag = jnp.dot(interior[low, :], trace, preferred_element_type=jnp.float32)
-        point = cells_row[...] == first + begin + lax.broadcasted_iota(jnp.int32, (ROWS, RHS), 0)
-        real = real * field_scale + point.astype(jnp.float32)
-        imag = imag * field_scale
-        real_b = real.astype(jnp.bfloat16)
-        imag_b = imag.astype(jnp.bfloat16)
-        minus_b = (-real).astype(jnp.bfloat16)
-        lu[rows, :NSRC] = real_b[:, :NSRC]
-        lu[rows, NSRC:] = imag_b[:, :NSRC]
-        ru[rows, :NSRC] = imag_b[:, :NSRC]
-        ru[rows, NSRC:] = minus_b[:, :NSRC]
-        lv[rows, :NRCV] = real_b[:, NSRC:]
-        lv[rows, NRCV:] = imag_b[:, NSRC:]
-        rv[rows, :NRCV] = imag_b[:, NSRC:]
-        rv[rows, NRCV:] = minus_b[:, NSRC:]
+    for half, cells, left, right in ((0, source_cells, lu, ru), (1, receiver_cells, lv, rv)):
+        receive(SWEEPS - 1, half)
+
+        @pl.loop(0, BLOCKS)
+        def _(i):
+            begin = pl.multiple_of(i * ROWS, ROWS)
+            trace = inc[SWEEPS - 1, half].reshape(TRACE, NSRC)
+            rows = pl.ds(begin, ROWS)
+            real = jnp.dot(interior[rows, :], trace, preferred_element_type=jnp.float32)
+            low = pl.ds(pl.multiple_of(CELLS + i * ROWS, ROWS), ROWS)
+            imag = jnp.dot(interior[low, :], trace, preferred_element_type=jnp.float32)
+            point = cells[...] == first + begin + lax.broadcasted_iota(jnp.int32, (ROWS, NSRC), 0)
+            real = real * field_scale + point.astype(jnp.float32)
+            imag = imag * field_scale
+            left[rows, :NSRC] = real.astype(jnp.bfloat16)
+            left[rows, NSRC:] = imag.astype(jnp.bfloat16)
+            right[rows, :NSRC] = imag.astype(jnp.bfloat16)
+            right[rows, NSRC:] = (-real).astype(jnp.bfloat16)
 
     def term(owner, j):
         rows = pl.ds(pl.multiple_of(owner * ROWS, ROWS), ROWS)
@@ -231,22 +233,29 @@
             device_id_type=MESH,
         )
 
-    @pl.loop(0, BLOCKS)
-    def _(j):
-        send_a[0, j] = term((1 - chip) * 2 + 1 - core, j).astype(jnp.bfloat16)
-        to_sibling(0, j).start()
-
-    @pl.loop(0, BLOCKS)
-    def _(j):
+    def give(half, j):
+        owner = (1 - chip + half * (2 * chip - 1)) * 2 + 1 - core
+        send_a[half, j] = term(owner, j).astype(jnp.bfloat16)
+        to_sibling(half, j).start()
+
+    def pass_on(j):
         own = term((1 - chip) * 2 + core, j)
         to_sibling(0, j).wait_recv()
         send_y[j] = (own + recv_a[0, j].astype(jnp.float32)).astype(jnp.bfloat16)
         to_across(j).start()
 
+    give(0, 0)
+
+    @pl.loop(0, BLOCKS - 1)
+    def _(j):
+        give(0, j + 1)
+        pass_on(j)
+
+    pass_on(BLOCKS - 1)
+
     @pl.loop(0, BLOCKS)
     def _(j):
-        send_a[1, j] = term(chip * 2 + 1 - core, j).astype(jnp.bfloat16)
-        to_sibling(1, j).start()
+        give(1, j)
 
     @pl.loop(0, BLOCKS)
     def _(j):
@@ -266,7 +275,8 @@
 
             @pl.when(valid[face])
             def _():
-                outward(k, face).wait_send()
+                for half in range(2):
+                    outward(k, half, face).wait_send()
 
     @pl.loop(0, BLOCKS)
     def _(j):
@@ -277,10 +287,9 @@
 
 def local(impedance, interior_map, source_cells, receiver_cells):
     nsub = lax.axis_size("sub")
-    cells = jnp.concatenate([source_cells, receiver_cells])
     bf16 = jnp.bfloat16
     vmem = pl.BlockSpec(memory_space=pltpu.VMEM)
-    anywhere = pl.BlockSpec(memory_space=pl.ANY)
+    anywhere = pl.BlockSpec(memory_space=pltpu.HBM)
 
     def body(*refs):
         kernel(nsub, *refs)
@@ -295,8 +304,8 @@
             pltpu.VMEM((TRACE, TRACE), jnp.float32),
             pltpu.VMEM((TRACE, TRACE), bf16),
             pltpu.VMEM((2 * CELLS, TRACE), bf16),
-            pltpu.VMEM((SWEEPS, 2, FACES, RHS), bf16),
-            pltpu.VMEM((SWEEPS, 2, FACES, RHS), bf16),
+            pltpu.VMEM((SWEEPS, 2, 2, FACES, NSRC), bf16),
+            pltpu.VMEM((SWEEPS, 2, 2, FACES, NSRC), bf16),
             pltpu.VMEM((CELLS, RHS), bf16),
             pltpu.VMEM((CELLS, RHS), bf16),
             pltpu.VMEM((CELLS, RHS), bf16),
@@ -306,17 +315,17 @@
             pltpu.VMEM((BLOCKS, ROWS, ROWS), bf16),
             pltpu.VMEM((BLOCKS, ROWS, ROWS), bf16),
             pltpu.SemaphoreType.DMA((3,)),
-            pltpu.SemaphoreType.DMA((SWEEPS, 6)),
-            pltpu.SemaphoreType.DMA((SWEEPS, 6)),
+            pltpu.SemaphoreType.DMA((SWEEPS, 2, 6)),
+            pltpu.SemaphoreType.DMA((SWEEPS, 2, 6)),
             pltpu.SemaphoreType.DMA((2, BLOCKS)),
             pltpu.SemaphoreType.DMA((2, BLOCKS)),
             pltpu.SemaphoreType.DMA((BLOCKS,)),
             pltpu.SemaphoreType.DMA((BLOCKS,)),
         ],
         compiler_params=pltpu.CompilerParams(
-            collective_id=0, has_side_effects=True, vmem_limit_bytes=60 * 1024 * 1024
+            collective_id=0, has_side_effects=True, vmem_limit_bytes=59 * 1024 * 1024
         ),
-    )(cells[None, :], cells[:, None], impedance[0, 0], interior_map[0, 0])
+    )(source_cells[None, :], receiver_cells[None, :], impedance[0, 0], interior_map[0, 0])
     return owned[None]
 
 

time: 63.2 us -> 56.2 us (0.89)
  the two profiles are of different devices: /device:TPU:164 before, /device:TPU:35 now
where the time goes in v2:
time: 56.2 us; the launch traced here: 56 us
  Pallas kernels  53.7 us (96%)
  local copies, waits for them, and re-layouts  2.31 us (4%)
    pallas_call x1, Pallas kernels, local(): pl.pallas_call(body, name='schwarz_hessian', out_shape=jax.ShapeDtypeStru...  53.7 us
    unnamed x1, local copies, waits for them, and re-layouts  2.31 us

profile of v2, /device:TPU:35, one launch (start us, length us, event | category | flops | bytes accessed | tf_op | source)
XLA Modules:
  0.0 56.0 jit_solution(14413250713631663343)
XLA Ops:
  0.0 53.7 %schwarz_hessian.1 = f32[256,1024]{1,0:T(8,128)} custom-call(s32[1,128]{1,0:T(1,128)} %bitcast.8, s32[1,128]{1,0:T(1,128)} %bitcast.9, f32[1280,1280]{1,0:T(8,128)} %bitcast.5, bf16[2048,1280]{1,0:T(8,128)(2,1)} %bitcast.6), custom_call_target="tpu_custom_call" | custom-call | tf_op jit(solution)/shard_map/schwarz_hessian/pallas_call | solution.py:297
  53.7 2.3 %copy.6 = f32[1,256,1024]{2,1,0:T(8,128)} copy(f32[1,256,1024]{2,1,0:T(8,128)} %bitcast.7) | data formatting | bytes 2097152

commit v3 on v2

--- a/solution.py
+++ b/solution.py
@@ -82,8 +82,6 @@
 
     fetch_z = pltpu.make_async_copy(z_hbm, zf, load_sem.at[2])
     fetch(0).start()
-    fetch_z.start()
-    fetch(1).start()
 
     barrier = pltpu.get_barrier_semaphore()
     greeted = jnp.int32(2)
@@ -147,6 +145,8 @@
         hot = jnp.concatenate([(column == lanes + i * NSRC).astype(jnp.float32) for i in range(CELLS // NSRC)], axis=1)
         if half == 0:
             fetch(0).wait()
+            fetch_z.start()
+            fetch(1).start()
         picked = jnp.dot(hot.astype(jnp.bfloat16), interior[:CELLS, :], preferred_element_type=jnp.float32)
         load = picked.T.astype(jnp.bfloat16)
         outb[0, half, 0] = load[:FACES]
@@ -323,7 +323,7 @@
             pltpu.SemaphoreType.DMA((BLOCKS,)),
         ],
         compiler_params=pltpu.CompilerParams(
-            collective_id=0, has_side_effects=True, vmem_limit_bytes=59 * 1024 * 1024
+            collective_id=0, has_side_effects=True, vmem_limit_bytes=52 * 1024 * 1024
         ),
     )(source_cells[None, :], receiver_cells[None, :], impedance[0, 0], interior_map[0, 0])
     return owned[None]

time: 56.2 us -> 54.5 us (0.970)
  Pallas kernels: 53.7 us -> 52.1 us
    pallas_call x1, Pallas kernels: 53.7 us -> 52.1 us  [local(): pl.pallas_call(body, name='schwarz_hessian', out_shape=jax.ShapeDtypeStru...]
    unnamed x1 -> x5, local copies, waits for them, and re-layouts: 2.31 us -> 2.28 us
where the time goes in v3:
time: 54.5 us; the launch traced here: 54.3 us
  Pallas kernels  52.1 us (96%)
  local copies, waits for them, and re-layouts  2.28 us (4%)
    pallas_call x1, Pallas kernels, local(): pl.pallas_call(body, name='schwarz_hessian', out_shape=jax.ShapeDtypeStru...  52.1 us
    unnamed x5, local copies, waits for them, and re-layouts  2.28 us

profile of v3, /device:TPU:35, one launch (start us, length us, event | category | flops | bytes accessed | tf_op | source)
XLA Modules:
  0.0 54.3 jit_solution(5184762532812835169)
XLA Ops:
  0.0 0.0 copy-start
  0.0 0.7 %copy-done = s32[128]{0:T(128)S(1)} copy-done((s32[128]{0:T(128)S(1)}, s32[128]{0:T(128)}, u32[]{:S(2)}) %copy-start) | copy-done | bytes 536
  0.7 0.0 copy-start.1
  0.7 0.7 %copy-done.1 = s32[128]{0:T(128)S(1)} copy-done((s32[128]{0:T(128)S(1)}, s32[128]{0:T(128)}, u32[]{:S(2)}) %copy-start.1) | copy-done | bytes 536
  1.3 52.1 %schwarz_hessian.1 = f32[256,1024]{1,0:T(8,128)S(1)} custom-call(s32[1,128]{1,0:T(1,128)S(1)} %bitcast.6, s32[1,128]{1,0:T(1,128)S(1)} %bitcast.7, f32[1280,1280]{1,0:T(8,128)} %bitcast.8, bf16[2048,1280]{1,0:T(8,128)(2,1)} %bitcast.9), custom_call_target="tpu_custom_call" | custom-call | tf_op jit(solution)/shard_map/schwarz_hessian/pallas_call | solution.py:297
  53.4 1.0 %copy.6 = f32[1,256,1024]{2,1,0:T(8,128)} copy(f32[1,256,1024]{2,1,0:T(8,128)S(1)} %bitcast.5) | data formatting | bytes 2097152
Async XLA Ops:
  0.0 0.7 %copy-start = (s32[128]{0:T(128)S(1)}, s32[128]{0:T(128)}, u32[]{:S(2)}) copy-start(s32[128]{0:T(128)} %param.6) | copy-start | bytes 1540
  0.7 0.7 %copy-start.1 = (s32[128]{0:T(128)S(1)}, s32[128]{0:T(128)}, u32[]{:S(2)}) copy-start(s32[128]{0:T(128)} %param.7) | copy-start | bytes 1540

commit v4 on v3

--- a/solution.py
+++ b/solution.py
@@ -147,14 +147,18 @@
             fetch(0).wait()
             fetch_z.start()
             fetch(1).start()
-        picked = jnp.dot(hot.astype(jnp.bfloat16), interior[:CELLS, :], preferred_element_type=jnp.float32)
-        load = picked.T.astype(jnp.bfloat16)
-        outb[0, half, 0] = load[:FACES]
-        outb[0, half, 1] = load[FACES:]
-        if half == 0:
-            pl.semaphore_wait(barrier, greeted)
-        for face in ORDER:
-            send(0, half, face)
+        hot = hot.astype(jnp.bfloat16)
+        for axis in (1, 0, 2):
+            begin = BEGINS[2 * axis]
+            count = COUNTS[2 * axis] * 2
+            for part in range(2):
+                columns = slice(part * FACES + begin, part * FACES + begin + count)
+                picked = jnp.dot(hot, interior[:CELLS, columns], preferred_element_type=jnp.float32)
+                outb[0, half, part, begin : begin + count, :] = picked.T.astype(jnp.bfloat16)
+            if half == 0 and axis == 1:
+                pl.semaphore_wait(barrier, greeted)
+            send(0, half, 2 * axis)
+            send(0, half, 2 * axis + 1)
 
     fetch_z.wait()
 
@@ -244,14 +248,10 @@
         send_y[j] = (own + recv_a[0, j].astype(jnp.float32)).astype(jnp.bfloat16)
         to_across(j).start()
 
-    give(0, 0)
-
-    @pl.loop(0, BLOCKS - 1)
-    def _(j):
-        give(0, j + 1)
+    @pl.loop(0, BLOCKS)
+    def _(j):
+        give(0, j)
         pass_on(j)
-
-    pass_on(BLOCKS - 1)
 
     @pl.loop(0, BLOCKS)
     def _(j):

time: 54.5 us -> 53.9 us (0.989)
  Pallas kernels: 52.1 us -> 51.5 us
    pallas_call x1, Pallas kernels: 52.1 us -> 51.5 us  [local(): pl.pallas_call(body, name='schwarz_hessian', out_shape=jax.ShapeDtypeStru...]
where the time goes in v4:
time: 53.9 us; the launch traced here: 53.7 us
  Pallas kernels  51.5 us (96%)
  local copies, waits for them, and re-layouts  2.28 us (4%)
    pallas_call x1, Pallas kernels, local(): pl.pallas_call(body, name='schwarz_hessian', out_shape=jax.ShapeDtypeStru...  51.5 us
    unnamed x5, local copies, waits for them, and re-layouts  2.28 us

profile of v4, /device:TPU:35, one launch (start us, length us, event | category | flops | bytes accessed | tf_op | source)
XLA Modules:
  0.0 53.7 jit_solution(12792370510690319803)
XLA Ops:
  0.0 0.0 copy-start
  0.0 0.7 %copy-done = s32[128]{0:T(128)S(1)} copy-done((s32[128]{0:T(128)S(1)}, s32[128]{0:T(128)}, u32[]{:S(2)}) %copy-start) | copy-done | bytes 536
  0.7 0.0 copy-start.1
  0.7 0.7 %copy-done.1 = s32[128]{0:T(128)S(1)} copy-done((s32[128]{0:T(128)S(1)}, s32[128]{0:T(128)}, u32[]{:S(2)}) %copy-start.1) | copy-done | bytes 536
  1.3 51.5 %schwarz_hessian.1 = f32[256,1024]{1,0:T(8,128)S(1)} custom-call(s32[1,128]{1,0:T(1,128)S(1)} %bitcast.6, s32[1,128]{1,0:T(1,128)S(1)} %bitcast.7, f32[1280,1280]{1,0:T(8,128)} %bitcast.8, bf16[2048,1280]{1,0:T(8,128)(2,1)} %bitcast.9), custom_call_target="tpu_custom_call" | custom-call | tf_op jit(solution)/shard_map/schwarz_hessian/pallas_call | solution.py:297
  52.8 1.0 %copy.6 = f32[1,256,1024]{2,1,0:T(8,128)} copy(f32[1,256,1024]{2,1,0:T(8,128)S(1)} %bitcast.5) | data formatting | bytes 2097152
Async XLA Ops:
  0.0 0.7 %copy-start = (s32[128]{0:T(128)S(1)}, s32[128]{0:T(128)}, u32[]{:S(2)}) copy-start(s32[128]{0:T(128)} %param.6) | copy-start | bytes 1540
  0.7 0.7 %copy-start.1 = (s32[128]{0:T(128)S(1)}, s32[128]{0:T(128)}, u32[]{:S(2)}) copy-start(s32[128]{0:T(128)} %param.7) | copy-start | bytes 1540
